TPU v7x, 512 devices: a whole 4x4x16 slice. The times are simulated.
512 devices in a mesh: rep: 16 (over x, z_lo), mp: 32 (over z_hi, y, core).
Axes of the slice: x: 4, y: 4, z: 16 (z_hi: 4, z_lo: 4; z = z_hi * 4 + z_lo), core: 2. Of those that a mesh axis runs over, the one named last changes fastest.
Arguments:
- dense_feats: bfloat16 [65536, 13], P(('rep', 'mp')), may hold values from -6 to 6
- bag_counts: int32 [65536, 32, 64], P('rep', 'mp'), may hold values from 0 to 2
- emb_rows: bfloat16 [32, 64, 256], P('mp'), may hold values from -0.625 to 0.625
- v_emb: bfloat16 [8192, 256], P('mp'), may hold values from -0.0625 to 0.0625
- u_emb: bfloat16 [256, 8192], P(None, 'mp'), may hold values from -0.375 to 0.375
- b_emb: bfloat16 [8192], P('mp'), may hold values from -3 to 3
- v_bot: bfloat16 [256, 256], replicated, may hold values from -0.375 to 0.375
- u_bot: bfloat16 [256, 256], replicated, may hold values from -0.375 to 0.375
- b_bot: bfloat16 [256], replicated, may hold values from -3 to 3
- w_first: bfloat16 [13, 1024], replicated, may hold values from -1.75 to 1.75
- b_first: bfloat16 [1024], replicated, may hold values from -3 to 3
- w_second: bfloat16 [1024, 256], replicated, may hold values from -0.1875 to 0.1875
- b_second: bfloat16 [256], replicated, may hold values from -3 to 3
- cot_cross: bfloat16 [65536, 8192], P(('rep', 'mp')), may hold values from -24 to 24
- cot_bottom: bfloat16 [65536, 256], P(('rep', 'mp')), may hold values from -6 to 6
Outputs:
- cross_emb: bfloat16 [65536, 8192], P(('rep', 'mp'))
- cross_bot: bfloat16 [65536, 256], P(('rep', 'mp'))
- grad_table: bfloat16 [32, 64, 256], P('mp')
- grad_v_emb: bfloat16 [8192, 256], P('mp')
- grad_u_emb: bfloat16 [256, 8192], P(None, 'mp')
- grad_b_emb: bfloat16 [8192], P('mp')
- grad_v_bot: bfloat16 [256, 256], replicated
- grad_u_bot: bfloat16 [256, 256], replicated
- grad_b_bot: bfloat16 [256], replicated
- grad_w_first: bfloat16 [13, 1024], replicated
- grad_b_first: bfloat16 [1024], replicated
- grad_w_second: bfloat16 [1024, 256], replicated
- grad_b_second: bfloat16 [256], replicated
Inputs may be any that keep to these rules, and one draw needn't show every extreme that they name: bag_counts[s, t, j] is how often row j of table t occurs in the bag of sample s.
All inputs are finite; a program needn't handle non-finite values.
Results may differ from a plain program's by a relative error of at most 0.029.
Values may be sent and summed in bfloat16 or wider, within the bound.
A program may use at most 64 MiB of HBM per device.

v0:
```python
import math
import jax
import jax.numpy as jnp
from jax import lax
from jax.sharding import PartitionSpec as P


def silu_slope(inputs):
    gate_value = jax.nn.sigmoid(inputs)
    return gate_value * (1.0 + inputs * (1.0 - gate_value))


def contract_rows(left_side, right_side):
    return lax.dot_general(
        left_side, right_side, (((0,), (0,)), ((), ())), preferred_element_type=jnp.float32
    )


def contract_cols(left_side, right_side):
    return lax.dot_general(
        left_side, right_side, (((1,), (1,)), ((), ())), preferred_element_type=jnp.float32
    )


def local(
    dense_feats,
    bag_counts,
    emb_rows,
    v_emb,
    u_emb,
    b_emb,
    v_bot,
    u_bot,
    b_bot,
    w_first,
    b_first,
    w_second,
    b_second,
    cot_cross,
    cot_bottom,
):
    group_size = lax.axis_size("mp")
    own_rows = dense_feats.shape[0]
    first_row = lax.axis_index("mp") * own_rows
    grad_scale = 1.0 / math.sqrt(own_rows * group_size * lax.axis_size("rep"))
    counts = bag_counts[:, 0, :].astype(jnp.bfloat16)
    pooled = jnp.dot(counts, emb_rows[0], preferred_element_type=jnp.float32).astype(jnp.bfloat16)
    partial_value = jnp.dot(pooled, v_emb, preferred_element_type=jnp.float32)
    first_pre = jnp.dot(dense_feats, w_first, preferred_element_type=jnp.float32) + b_first.astype(
        jnp.float32
    )
    first_act = jax.nn.silu(first_pre).astype(jnp.bfloat16)
    second_pre = jnp.dot(first_act, w_second, preferred_element_type=jnp.float32) + b_second.astype(
        jnp.float32
    )
    bottom = jax.nn.silu(second_pre).astype(jnp.bfloat16)
    own_part = lax.dynamic_slice_in_dim(partial_value, first_row, own_rows, 0) + jnp.dot(
        bottom, v_bot, preferred_element_type=jnp.float32
    )
    partial_value = lax.dynamic_update_slice_in_dim(partial_value, own_part, first_row, 0)
    low_rank = lax.psum(partial_value.astype(jnp.bfloat16), "mp")
    lift_emb = jnp.dot(low_rank, u_emb, preferred_element_type=jnp.float32) + b_emb.astype(
        jnp.float32
    )
    pooled_full = pooled.astype(jnp.float32)
    cross_local = (pooled_full * (lift_emb + 1.0)).astype(jnp.bfloat16)
    cross_emb = lax.all_to_all(cross_local, "mp", split_axis=0, concat_axis=1, tiled=True)
    own_low = lax.dynamic_slice_in_dim(low_rank, first_row, own_rows, 0)
    lift_bottom = jnp.dot(own_low, u_bot, preferred_element_type=jnp.float32) + b_bot.astype(
        jnp.float32
    )
    bottom_full = bottom.astype(jnp.float32)
    cross_bot = (bottom_full * (lift_bottom + 1.0)).astype(jnp.bfloat16)
    cot_rows = lax.all_to_all(cot_cross, "mp", split_axis=1, concat_axis=0, tiled=True).astype(
        jnp.float32
    )
    d_lift = cot_rows * pooled_full
    d_lift_round = d_lift.astype(jnp.bfloat16)
    own_back = lax.psum_scatter(
        contract_cols(d_lift_round, u_emb).astype(jnp.bfloat16),
        "mp",
        scatter_dimension=0,
        tiled=True,
    ).astype(jnp.float32)
    cot_low = cot_bottom.astype(jnp.float32)
    d_bottom_lift = cot_low * bottom_full
    d_bottom_round = d_bottom_lift.astype(jnp.bfloat16)
    own_d_low = (own_back + contract_cols(d_bottom_round, u_bot)).astype(jnp.bfloat16)
    d_low = lax.all_gather(own_d_low, "mp", axis=0, tiled=True)
    d_pooled = (cot_rows * (lift_emb + 1.0) + contract_cols(d_low, v_emb)).astype(jnp.bfloat16)
    grad_table = grad_scale * contract_rows(counts, d_pooled)
    grad_v = grad_scale * contract_rows(pooled, d_low)
    grad_u = grad_scale * contract_rows(low_rank, d_lift_round)
    grad_b = grad_scale * jnp.sum(d_lift, axis=0)
    d_bottom = cot_low * (lift_bottom + 1.0) + contract_cols(own_d_low, v_bot)
    grad_vb = grad_scale * contract_rows(bottom, own_d_low)
    grad_ub = grad_scale * contract_rows(own_low, d_bottom_round)
    grad_bb = grad_scale * jnp.sum(d_bottom_lift, axis=0)
    d_second = d_bottom * silu_slope(second_pre)
    d_second_round = d_second.astype(jnp.bfloat16)
    grad_ws = grad_scale * contract_rows(first_act, d_second_round)
    grad_bs = grad_scale * jnp.sum(d_second, axis=0)
    d_first = contract_cols(d_second_round, w_second) * silu_slope(first_pre)
    d_first_round = d_first.astype(jnp.bfloat16)
    grad_wf = grad_scale * contract_rows(dense_feats, d_first_round)
    grad_bf = grad_scale * jnp.sum(d_first, axis=0)
    dense_sums = lax.psum(
        (grad_wf, grad_bf, grad_ws, grad_bs, grad_vb, grad_ub, grad_bb), ("rep", "mp")
    )
    table_sums = (
        lax.psum(grad_table.astype(jnp.bfloat16), "rep").astype(jnp.float32),
        lax.psum(grad_v.astype(jnp.bfloat16), "rep").astype(jnp.float32),
        lax.psum(grad_u.astype(jnp.bfloat16), "rep").astype(jnp.float32),
        lax.psum(grad_b.astype(jnp.bfloat16), "rep").astype(jnp.float32),
    )
    return (
        cross_emb,
        cross_bot,
        table_sums[0][None].astype(jnp.bfloat16),
        table_sums[1].astype(jnp.bfloat16),
        table_sums[2].astype(jnp.bfloat16),
        table_sums[3].astype(jnp.bfloat16),
        dense_sums[4].astype(jnp.bfloat16),
        dense_sums[5].astype(jnp.bfloat16),
        dense_sums[6].astype(jnp.bfloat16),
        dense_sums[0].astype(jnp.bfloat16),
        dense_sums[1].astype(jnp.bfloat16),
        dense_sums[2].astype(jnp.bfloat16),
        dense_sums[3].astype(jnp.bfloat16),
    )


def solution(mesh):
    return jax.shard_map(
        local,
        mesh=mesh,
        in_specs=(
            P(("rep", "mp"), None),
            P("rep", "mp", None),
            P("mp", None, None),
            P("mp", None),
            P(None, "mp"),
            P("mp"),
            P(),
            P(),
            P(),
            P(),
            P(),
            P(),
            P(),
            P(("rep", "mp"), None),
            P(("rep", "mp"), None),
        ),
        out_specs=(
            P(("rep", "mp"), None),
            P(("rep", "mp"), None),
            P("mp", None, None),
            P("mp", None),
            P(None, "mp"),
            P("mp"),
            P(),
            P(),
            P(),
            P(),
            P(),
            P(),
            P(),
        ),
        check_vma=False,
    )
```

profile of v0, /device:TPU:8, one launch (start us, length us, event | category | flops | bytes accessed | tf_op | source)
XLA Modules:
  0.0 923.8 jit_solution(9754976400988497330)
XLA Ops:
  7.2 3.2 copy.33
  10.4 18.5 %all-to-all-start.1 = ((bf16[128,32,256]{2,0,1:T(8,128)(2,1)}), bf16[128,32,256]{2,0,1:T(8,128)(2,1)}, u32[]{:S(2)}, u32[]{:S(2)}) async-start(bf16[128,32,256]{2,0,1:T(8,128)(2,1)} %bitcast.58), calls=%async_computation.1 | async-start | bytes 4194304 | tf_op jit(solution)/shard_map/all_to_all | solution.py:74
  29.1 0.3 convolution_add_fusion.2
  29.4 0.8 copy-done.5
  30.2 1.0 fusion.22
  31.1 2.0 convolution_convert_fusion.1
  33.1 0.7 fusion.35
  33.9 0.2 copy-done.9
  34.2 1.5 convert_element_type.134
  35.8 0.6 copy-done.16
  36.4 399.7 %all-reduce.7.cloned.1.call-done = bf16[4096,256]{1,0:T(8,128)(2,1)} async-done(((bf16[4096,256]{1,0:T(8,128)(2,1)}), bf16[4096,256]{1,0:T(8,128)(2,1)}) %all-reduce.7.cloned.1.call-update) | async-done | bytes 2097168 | tf_op jit(solution)/shard_map/psum | solution.py:61
  436.1 6.4 bitcast_multiply_fusion
  442.6 1.3 copy-done.1
  443.9 2.1 convolution_convert_fusion
  446.1 21.6 %all-to-all-start = ((bf16[32,128,256]{2,1,0:T(8,128)(2,1)}), bf16[32,128,256]{2,1,0:T(8,128)(2,1)}, u32[]{:S(2)}, u32[]{:S(2)}) async-start(bf16[32,128,256]{2,1,0:T(8,128)(2,1)} %bitcast.59), calls=%async_computation | async-start | bytes 4194304 | tf_op jit(solution)/shard_map/all_to_all | solution.py:67
  467.7 151.9 %reduce-scatter.2.cloned.1.call-done = bf16[128,256]{1,0:T(8,128)(2,1)} async-done(((bf16[4096,256]{1,0:T(8,128)(2,1)}), bf16[128,256]{1,0:T(8,128)(2,1)}) %reduce-scatter.2.cloned.1.call-update) | async-done | bytes 65552 | tf_op jit(solution)/shard_map/reduce_scatter | solution.py:79
  619.7 1.7 fusion.11
  621.4 1.1 convolution_multiply_fusion.2
  622.5 1.6 fusion.21
  624.2 3.7 fusion.7
  627.9 0.2 convolution_multiply_fusion.3
  628.1 0.2 fusion.34
  628.4 0.4 fusion.33
  628.9 1.4 convolution_multiply_fusion
  630.3 114.5 %all-reduce.10 = (bf16[256,256]{1,0:T(8,128)(2,1)}, bf16[256,256]{1,0:T(8,128)(2,1)}, bf16[256]{0:T(256)(128)(2,1)}, bf16[13,1024]{1,0:T(8,128)(2,1)}, bf16[1024...) all-reduce(f32[256,256]{1,0:T(8,128)S(1)} %convolution_multiply_fus, ...), channel_id=1, replica_groups=mesh['rep'=16,'mp'=32] {'rep','mp'}, use_global_device_ids=true, to_apply=%region_7.8 | all-reduce | flops 408064 | bytes 2448384 | tf_op jit(solution)/shard_map/psum | solution.py:107
  744.8 3.0 fusion.6
  747.8 4.5 fusion.15
  752.3 78.6 %all-reduce.1 = (bf16[1,64,256]{2,1,0:T(8,128)(2,1)}, bf16[256]{0:T(256)(128)(2,1)}) all-reduce(bf16[1,64,256]{2,1,0:T(8,128)(2,1)S(1)} %fusion.15, bf16[256]{0:T(256)(128)(2,1)S(1)} %multiply_convert_fusion.2), channel_id=1, replica_groups=mesh['rep'=16,'mp'=32] {'rep'}, use_global_device_ids=true, to_apply=%region_2.3 | all-reduce | flops 16640 | bytes 66560 | tf_op jit(solution)/shard_map/psum | solution.py:111
  830.9 3.1 copy.31
  834.0 80.1 %all-reduce.9.cloned.1.call-done = (bf16[256,256]{1,0:T(8,128)(2,1)}, bf16[256,256]{1,0:T(8,128)(2,1)}) async-done(((bf16[256,256]{1,0:T(8,128)(2,1)}, bf16[256,256]{1,0:T(8,128)(2,1)}), (bf16[256,256]{1,0:T(8,128)(2,1)}, bf16[256,256]{1,0:T(8,128)(2,1)})) %all-reduce.9.cloned.1.call-update) | async-done | bytes 262160 | tf_op jit(solution)/shard_map/psum | solution.py:112
  914.1 1.6 copy.52
  915.7 1.6 copy.53
  (55 shorter events, 0.7 us)
Async XLA Ops:
  7.2 23.0 %copy-start = (bf16[1024,256]{1,0:T(8,128)(2,1)S(1)}, bf16[1024,256]{1,0:T(8,128)(2,1)}, u32[]{:S(2)}) copy-start(bf16[1024,256]{1,0:T(8,128)(2,1)} %param.26) | copy-start | bytes 1572868
  10.4 18.6 %copy-start.15 = (bf16[256]{0:T(256)(128)(2,1)S(1)}, bf16[256]{0:T(256)(128)(2,1)}, u32[]{:S(2)}) copy-start(bf16[256]{0:T(256)(128)(2,1)} %param.27) | copy-start | bytes 1540
  10.4 18.6 %copy-start.14 = (bf16[1024]{0:T(1024)(128)(2,1)S(1)}, bf16[1024]{0:T(1024)(128)(2,1)}, u32[]{:S(2)}) copy-start(bf16[1024]{0:T(1024)(128)(2,1)} %param.25) | copy-start | bytes 6148
  10.4 18.7 %copy-start.12 = (bf16[13,1024]{1,0:T(8,128)(2,1)S(1)}, bf16[13,1024]{1,0:T(8,128)(2,1)}, u32[]{:S(2)}) copy-start(bf16[13,1024]{1,0:T(8,128)(2,1)} %param.24) | copy-start | bytes 79876
  10.4 18.7 %copy-start.13 = (bf16[128,13]{0,1:T(8,128)(2,1)S(1)}, bf16[128,13]{0,1:T(8,128)(2,1)}, u32[]{:S(2)}) copy-start(bf16[128,13]{0,1:T(8,128)(2,1)} %param.15) | copy-start | bytes 9988
  10.4 19.7 %copy-start.8 = (bf16[128,256]{1,0:T(8,128)(2,1)S(1)}, bf16[128,256]{1,0:T(8,128)(2,1)}, u32[]{:S(2)}) copy-start(bf16[128,256]{1,0:T(8,128)(2,1)} %param.29) | copy-start | bytes 196612
  10.4 425.7 %all-to-all-start.1 = ((bf16[128,32,256]{2,0,1:T(8,128)(2,1)}), bf16[128,32,256]{2,0,1:T(8,128)(2,1)}, u32[]{:S(2)}, u32[]{:S(2)}) async-start(bf16[128,32,256]{2,0,1:T(8,128)(2,1)} %bitcast.58), calls=%async_computation.1 | async-start | bytes 4194304 | tf_op jit(solution)/shard_map/all_to_all | solution.py:74
  29.0 2.1 copy-start.11
  29.0 407.2 %all-reduce.7.cloned.1.call-start = ((), (), s32[]{:S(2)}) async-start(), calls=%async_computation.3 | async-start | bytes 4194304 | tf_op jit(solution)/shard_map/psum | solution.py:61
  29.4 0.8 copy-start.5
  31.1 2.0 copy-start.4
  33.1 0.9 copy-start.9
  35.8 0.7 copy-start.16
  35.8 400.4 %copy-start.3 = (bf16[256,256]{1,0:T(8,128)(2,1)S(1)}, bf16[256,256]{1,0:T(8,128)(2,1)}, u32[]{:S(2)}) copy-start(bf16[256,256]{1,0:T(8,128)(2,1)} %param.19) | copy-start | bytes 393220
  35.8 583.9 %reduce-scatter.2.cloned.1.call-start = ((), (), s32[]{:S(2)}) async-start(), calls=%async_computation.4 | async-start | bytes 2162688 | tf_op jit(solution)/shard_map/reduce_scatter | solution.py:79
  442.6 1.3 copy-start.1
  446.0 173.6 %copy-start.7 = (bf16[256,256]{1,0:T(8,128)(2,1)S(1)}, bf16[256,256]{1,0:T(8,128)(2,1)}, u32[]{:S(2)}) copy-start(bf16[256,256]{1,0:T(8,128)(2,1)} %param.22) | copy-start | bytes 393220
  446.1 175.3 %copy-start.17 = (bf16[256]{0:T(256)(128)(2,1)S(1)}, bf16[256]{0:T(256)(128)(2,1)}, u32[]{:S(2)}) copy-start(bf16[256]{0:T(256)(128)(2,1)} %param.23) | copy-start | bytes 1540
  446.1 384.9 %all-to-all-start = ((bf16[32,128,256]{2,1,0:T(8,128)(2,1)}), bf16[32,128,256]{2,1,0:T(8,128)(2,1)}, u32[]{:S(2)}, u32[]{:S(2)}) async-start(bf16[32,128,256]{2,1,0:T(8,128)(2,1)} %bitcast.59), calls=%async_computation | async-start | bytes 4194304 | tf_op jit(solution)/shard_map/all_to_all | solution.py:67
  467.7 277.1 %all-gather.2.cloned.1.call-start = ((), (), s32[]{:S(2)}) async-start(), calls=%async_computation.5 | async-start | bytes 2162688 | tf_op jit(solution)/shard_map/all_gather | solution.py:89
  621.4 292.8 %all-reduce.9.cloned.1.call-start = ((), (), s32[]{:S(2)}) async-start(), calls=%async_computation.6 | async-start | bytes 524288 | tf_op jit(solution)/shard_map/psum | solution.py:112
  624.2 3.7 copy-start.2
  624.2 4.0 copy-start.10
  624.2 4.0 copy-start.18
  624.2 4.2 copy-start.6
Sparse Core Ops, SparseCore 0:
  35.9 400.1 all-reduce.6
  446.2 173.4 reduce-scatter.1
  623.8 74.0 all-gather.1
  747.9 166.1 all-reduce.8
where the time goes:
time: 924 us
  waiting for transfers between devices  632 us (68%)
  blocking collectives  193 us (21%)
  starting transfers between devices  40.3 us (4%)
  matrix products  30.5 us (3%)
  between operations  14.1 us (2%)
  local copies, waits for them, and re-layouts  12.5 us (1%)
    psum x1, waiting for transfers between devices, local(): low_rank = lax.psum(partial_value.astype(jnp.bfloat16), 'mp')  400 us
    reduce_scatter x1, waiting for transfers between devices, local(): lax.psum_scatter(contract_cols(d_lift_round, u_emb).astype(jnp.bfloat16),...  152 us
    psum x1, blocking collectives, local(): lax.psum((grad_wf, grad_bf, grad_ws, grad_bs, grad_vb, grad_ub, grad_bb),...  115 us
    psum x1, waiting for transfers between devices, local(): lax.psum(grad_v.astype(jnp.bfloat16), 'rep').astype(jnp.float32)  80.1 us
    psum x1, blocking collectives, local(): lax.psum(grad_table.astype(jnp.bfloat16), 'rep').astype(jnp.float32)  78.6 us
    all_to_all x1, starting transfers between devices, local(): lax.all_to_all(cross_local, 'mp', split_axis=0, concat_axis=1, tiled=True)  21.6 us
    all_to_all x1, starting transfers between devices, local(): lax.all_to_all(cot_cross, 'mp', split_axis=1, concat_axis=0, tiled=True)  18.5 us
  transfers between devices with their start and end apart: 6, of which 3 were waited for; matrix products, arithmetic and copies ran while one was open for 3% of the time, Pallas kernels for 0%

commit v1 on v0

--- a/solution.py
+++ b/solution.py
@@ -3,6 +3,12 @@
 import jax.numpy as jnp
 from jax import lax
 from jax.sharding import PartitionSpec as P
+from jax.lax import all_gather
+
+
+def _divide_cubes(frame_in, named_axis):
+    response = jnp.sum(all_gather(frame_in, axis_name=named_axis), axis=0)
+    return response
 
 
 def silu_slope(inputs):
@@ -109,7 +115,7 @@
     )
     table_sums = (
         lax.psum(grad_table.astype(jnp.bfloat16), "rep").astype(jnp.float32),
-        lax.psum(grad_v.astype(jnp.bfloat16), "rep").astype(jnp.float32),
+        _divide_cubes(grad_v.astype(jnp.bfloat16), "rep").astype(jnp.float32),
         lax.psum(grad_u.astype(jnp.bfloat16), "rep").astype(jnp.float32),
         lax.psum(grad_b.astype(jnp.bfloat16), "rep").astype(jnp.float32),
     )

time: 924 us -> 1010 us (1.093)
  waiting for transfers between devices: 632 us -> 728 us
  starting transfers between devices: 40.3 us -> 28.3 us
    all_gather x1, waiting for transfers between devices: 0.01 us -> 148 us  [local(): d_low = lax.all_gather(own_d_low, 'mp', axis=0, tiled=True)]
    psum x1, waiting for transfers between devices: 80.1 us -> 51.2 us  [local(): lax.psum(grad_u.astype(jnp.bfloat16), 'rep').astype(jnp.float32)]
    reduce_scatter x1, waiting for transfers between devices: 152 us -> 128 us  [local(): lax.psum_scatter(contract_cols(d_lift_round, u_emb).astype(jnp.bfloat16),...]
    all_to_all x1, starting transfers between devices: 21.6 us -> 9.54 us  [local(): lax.all_to_all(cross_local, 'mp', split_axis=0, concat_axis=1, tiled=True)]
  transfers between devices with their start and end apart: 6 -> 7, of which waited for: 3 -> 4; matrix products, arithmetic and copies ran while one was open for 3% -> 3% of each run, Pallas kernels for 0% -> 0%
where the time goes in v1:
time: 1010 us; the launch traced here: 1000 us
  waiting for transfers between devices  728 us (72%)
  blocking collectives  189 us (19%)
  matrix products  29.2 us (3%)
  starting transfers between devices  28.3 us (3%)
  between operations  14.1 us (1%)
  local copies, waits for them, and re-layouts  11.2 us (1%)
    psum x1, waiting for transfers between devices, local(): low_rank = lax.psum(partial_value.astype(jnp.bfloat16), 'mp')  401 us
    all_gather x1, waiting for transfers between devices, local(): d_low = lax.all_gather(own_d_low, 'mp', axis=0, tiled=True)  148 us
    reduce_scatter x1, waiting for transfers between devices, local(): lax.psum_scatter(contract_cols(d_lift_round, u_emb).astype(jnp.bfloat16),...  128 us
    psum x1, blocking collectives, local(): lax.psum((grad_wf, grad_bf, grad_ws, grad_bs, grad_vb, grad_ub, grad_bb),...  111 us
    psum x1, blocking collectives, local(): lax.psum(grad_table.astype(jnp.bfloat16), 'rep').astype(jnp.float32)  77.8 us
    psum x1, waiting for transfers between devices, local(): lax.psum(grad_u.astype(jnp.bfloat16), 'rep').astype(jnp.float32)  51.2 us
  transfers between devices with their start and end apart: 7, of which 4 were waited for; matrix products, arithmetic and copies ran while one was open for 3% of the time, Pallas kernels for 0%

profile of v1, /device:TPU:8, one launch (start us, length us, event | category | flops | bytes accessed | tf_op | source)
XLA Modules:
  0.0 1004.4 jit_solution(12979561957651060080)
XLA Ops:
  7.2 3.2 copy.33
  10.4 18.5 %all-to-all-start.1 = ((bf16[128,32,256]{2,0,1:T(8,128)(2,1)}), bf16[128,32,256]{2,0,1:T(8,128)(2,1)}, u32[]{:S(2)}, u32[]{:S(2)}) async-start(bf16[128,32,256]{2,0,1:T(8,128)(2,1)} %bitcast.59), calls=%async_computation.1 | async-start | bytes 4194304 | tf_op jit(solution)/shard_map/all_to_all | solution.py:80
  29.1 0.2 convolution_add_fusion.2
  29.4 0.8 copy-done.6
  30.2 1.0 fusion.22
  31.1 2.0 convolution_convert_fusion.1
  33.1 0.7 fusion.35
  34.2 1.5 convert_element_type.136
  35.8 0.6 copy-done.17
  36.4 400.6 %all-reduce.6.cloned.1.call-done = bf16[4096,256]{1,0:T(8,128)(2,1)} async-done(((bf16[4096,256]{1,0:T(8,128)(2,1)}), bf16[4096,256]{1,0:T(8,128)(2,1)}) %all-reduce.6.cloned.1.call-update) | async-done | bytes 2097168 | tf_op jit(solution)/shard_map/psum | solution.py:67
  437.0 6.4 bitcast_multiply_fusion
  443.5 1.4 copy-done.1
  444.8 2.1 convolution_convert_fusion
  447.0 128.1 %reduce-scatter.2.cloned.1.call-done = bf16[128,256]{1,0:T(8,128)(2,1)} async-done(((bf16[4096,256]{1,0:T(8,128)(2,1)}), bf16[128,256]{1,0:T(8,128)(2,1)}) %reduce-scatter.2.cloned.1.call-update) | async-done | bytes 65552 | tf_op jit(solution)/shard_map/reduce_scatter | solution.py:85
  575.1 1.7 fusion.11
  576.8 9.5 all-to-all-start
  586.4 148.3 %all-gather.4.cloned.1.call-done = bf16[4096,256]{1,0:T(8,128)(2,1)} async-done(((bf16[128,256]{1,0:T(8,128)(2,1)}), bf16[4096,256]{1,0:T(8,128)(2,1)}) %all-gather.4.cloned.1.call-update) | async-done | bytes 2097168 | tf_op jit(solution)/shard_map/all_gather | solution.py:95
  734.7 3.0 fusion.6
  737.9 1.1 convolution_multiply_fusion.2
  738.9 1.6 fusion.21
  740.6 3.7 fusion.7
  744.6 0.2 fusion.34
  744.8 0.4 fusion.33
  745.3 0.3 copy-done.8
  745.6 0.4 convolution_multiply_fusion
  746.0 111.5 %all-reduce.9 = (bf16[256,256]{1,0:T(8,128)(2,1)}, bf16[256,256]{1,0:T(8,128)(2,1)}, bf16[256]{0:T(256)(128)(2,1)}, bf16[13,1024]{1,0:T(8,128)(2,1)}, bf16[1024]...) all-reduce(f32[256,256]{1,0:T(8,128)S(1)} %convolution_multiply_fus, ...), channel_id=1, replica_groups=mesh['rep'=16,'mp'=32] {'rep','mp'}, use_global_device_ids=true, to_apply=%region_7.8 | all-reduce | flops 408064 | bytes 2448384 | tf_op jit(solution)/shard_map/psum | solution.py:113
  857.5 4.1 fusion.15
  861.6 77.8 %all-reduce.1 = (bf16[1,64,256]{2,1,0:T(8,128)(2,1)}, bf16[256]{0:T(256)(128)(2,1)}) all-reduce(bf16[1,64,256]{2,1,0:T(8,128)(2,1)S(1)} %fusion.15, bf16[256]{0:T(256)(128)(2,1)S(1)} %multiply_convert_fusion.2), channel_id=1, replica_groups=mesh['rep'=16,'mp'=32] {'rep'}, use_global_device_ids=true, to_apply=%region_2.3 | all-reduce | flops 16640 | bytes 66560 | tf_op jit(solution)/shard_map/psum | solution.py:117
  939.4 3.1 copy.31
  942.5 2.6 reduce_sum.48
  945.1 51.2 %all-reduce.8.cloned.1.call-done = bf16[256,256]{1,0:T(8,128)(2,1)} async-done(((bf16[256,256]{1,0:T(8,128)(2,1)}), bf16[256,256]{1,0:T(8,128)(2,1)}) %all-reduce.8.cloned.1.call-update) | async-done | bytes 131088 | tf_op jit(solution)/shard_map/psum | solution.py:119
  996.3 1.6 copy.51
  (60 shorter events, 1.1 us)
Async XLA Ops:
  7.2 23.0 %copy-start = (bf16[1024,256]{1,0:T(8,128)(2,1)S(1)}, bf16[1024,256]{1,0:T(8,128)(2,1)}, u32[]{:S(2)}) copy-start(bf16[1024,256]{1,0:T(8,128)(2,1)} %param.26) | copy-start | bytes 1572868
  10.4 18.6 %copy-start.16 = (bf16[256]{0:T(256)(128)(2,1)S(1)}, bf16[256]{0:T(256)(128)(2,1)}, u32[]{:S(2)}) copy-start(bf16[256]{0:T(256)(128)(2,1)} %param.27) | copy-start | bytes 1540
  10.4 18.6 %copy-start.15 = (bf16[1024]{0:T(1024)(128)(2,1)S(1)}, bf16[1024]{0:T(1024)(128)(2,1)}, u32[]{:S(2)}) copy-start(bf16[1024]{0:T(1024)(128)(2,1)} %param.25) | copy-start | bytes 6148
  10.4 18.7 %copy-start.13 = (bf16[13,1024]{1,0:T(8,128)(2,1)S(1)}, bf16[13,1024]{1,0:T(8,128)(2,1)}, u32[]{:S(2)}) copy-start(bf16[13,1024]{1,0:T(8,128)(2,1)} %param.24) | copy-start | bytes 79876
  10.4 18.7 %copy-start.14 = (bf16[128,13]{0,1:T(8,128)(2,1)S(1)}, bf16[128,13]{0,1:T(8,128)(2,1)}, u32[]{:S(2)}) copy-start(bf16[128,13]{0,1:T(8,128)(2,1)} %param.15) | copy-start | bytes 9988
  10.4 19.7 %copy-start.10 = (bf16[128,256]{1,0:T(8,128)(2,1)S(1)}, bf16[128,256]{1,0:T(8,128)(2,1)}, u32[]{:S(2)}) copy-start(bf16[128,256]{1,0:T(8,128)(2,1)} %param.29) | copy-start | bytes 196612
  10.4 426.6 %all-to-all-start.1 = ((bf16[128,32,256]{2,0,1:T(8,128)(2,1)}), bf16[128,32,256]{2,0,1:T(8,128)(2,1)}, u32[]{:S(2)}, u32[]{:S(2)}) async-start(bf16[128,32,256]{2,0,1:T(8,128)(2,1)} %bitcast.59), calls=%async_computation.1 | async-start | bytes 4194304 | tf_op jit(solution)/shard_map/all_to_all | solution.py:80
  29.0 2.1 copy-start.12
  29.0 408.0 %all-reduce.6.cloned.1.call-start = ((), (), s32[]{:S(2)}) async-start(), calls=%async_computation.3 | async-start | bytes 4194304 | tf_op jit(solution)/shard_map/psum | solution.py:67
  29.4 0.8 copy-start.6
  31.1 2.0 copy-start.5
  33.1 0.9 copy-start.11
  35.7 0.7 copy-start.17
  35.7 401.3 %copy-start.4 = (bf16[256,256]{1,0:T(8,128)(2,1)S(1)}, bf16[256,256]{1,0:T(8,128)(2,1)}, u32[]{:S(2)}) copy-start(bf16[256,256]{1,0:T(8,128)(2,1)} %param.19) | copy-start | bytes 393220
  35.8 539.3 %reduce-scatter.2.cloned.1.call-start = ((), (), s32[]{:S(2)}) async-start(), calls=%async_computation.4 | async-start | bytes 2162688 | tf_op jit(solution)/shard_map/reduce_scatter | solution.py:85
  443.4 1.4 copy-start.1
  446.9 128.2 %copy-start.9 = (bf16[256,256]{1,0:T(8,128)(2,1)S(1)}, bf16[256,256]{1,0:T(8,128)(2,1)}, u32[]{:S(2)}) copy-start(bf16[256,256]{1,0:T(8,128)(2,1)} %param.22) | copy-start | bytes 393220
  446.9 287.8 %all-gather.4.cloned.1.call-start = ((), (), s32[]{:S(2)}) async-start(), calls=%async_computation.5 | async-start | bytes 2162688 | tf_op jit(solution)/shard_map/all_gather | solution.py:95
  576.8 362.6 %all-to-all-start = ((bf16[32,128,256]{2,1,0:T(8,128)(2,1)}), bf16[32,128,256]{2,1,0:T(8,128)(2,1)}, u32[]{:S(2)}, u32[]{:S(2)}) async-start(bf16[32,128,256]{2,1,0:T(8,128)(2,1)} %bitcast.60), calls=%async_computation | async-start | bytes 4194304 | tf_op jit(solution)/shard_map/all_to_all | solution.py:73
  586.3 151.5 %copy-start.18 = (bf16[256]{0:T(256)(128)(2,1)S(1)}, bf16[256]{0:T(256)(128)(2,1)}, u32[]{:S(2)}) copy-start(bf16[256]{0:T(256)(128)(2,1)} %param.23) | copy-start | bytes 1540
  586.3 356.2 %all-gather.6.cloned.1.call-start = ((), (), s32[]{:S(2)}) async-start(), calls=%async_computation.7 | async-start | bytes 2228224 | tf_op jit(solution)/shard_map/all_gather | solution.py:10
  737.8 258.6 %all-reduce.8.cloned.1.call-start = ((), (), s32[]{:S(2)}) async-start(), calls=%async_computation.6 | async-start | bytes 262144 | tf_op jit(solution)/shard_map/psum | solution.py:119
  740.6 3.8 copy-start.3
  740.6 4.0 copy-start.19
  740.6 4.2 copy-start.7
  744.6 1.0 copy-start.8
  745.6 111.9 %copy-start.2 = (s32[4096,1,64]{0,2,1:T(8,128)S(1)}, s32[4096,1,64]{0,2,1:T(8,128)}, u32[]{:S(2)}) copy-start(s32[4096,1,64]{0,2,1:T(8,128)} %param.16) | copy-start | bytes 3145732
Sparse Core Ops, SparseCore 0:
  35.9 401.0 all-reduce.5
  447.1 127.9 reduce-scatter.1
  579.3 155.4 all-gather.3
  737.9 87.6 all-gather.5
  828.6 167.7 all-reduce.7
